TPU v7x, 32 devices: a whole 2x2x4 slice. The times are simulated.
32 devices in a mesh: wide: 8 (over y, x, core), narrow: 4 (over z).
Axes of the slice: x: 2, y: 2, z: 4, core: 2. Of those that a mesh axis runs over, the one named last changes fastest.
Arguments:
- states: bfloat16 [16384, 1024], P(('wide', 'narrow')), may hold values from -6 to 6
- applied: bfloat16 [16384, 1024], P(('wide', 'narrow')), may hold values from -6 to 6
- rotation: bfloat16 [2, 1024, 256], P(None, 'wide', 'narrow'), may hold values from -0.1875 to 0.1875
- ritz: float32 [2, 256], replicated, may hold values from 0.5 to 4
- potential: float32 [16384], P(('wide', 'narrow')), may hold values from 0.5 to 8
Outputs:
- rotated: bfloat16 [16384, 2, 256], P(('wide', 'narrow'))
- correction: bfloat16 [16384, 2, 256], P(('wide', 'narrow'))
- margin: float32 [2, 1024, 256], P(None, 'wide', 'narrow')
All inputs are finite; a program needn't handle non-finite values.
Results may differ from a plain program's by a relative error of at most 0.0095.
Values may be sent and summed in bfloat16 or wider, within the bound.
A program may use at most 64 MiB of HBM per device.

v0:
```python
import math
import jax
import jax.numpy as jnp
from jax import lax
from jax.sharding import PartitionSpec as P


def per_device(states, applied, rotation, ritz, potential):
    row_count = states.shape[0]
    total_rows = row_count * lax.axis_size("wide") * lax.axis_size("narrow")
    factor = 1.0 / math.sqrt(total_rows)
    contract = (((0,), (0,)), ((), ()))
    rotated_list = []
    correction_list = []
    margin_list = []
    for window in range(rotation.shape[0]):
        q_local = rotation[window]
        q_tall = lax.all_gather(q_local, "wide", axis=0, tiled=True)
        q_full = lax.all_gather(q_tall, "narrow", axis=1, tiled=True)
        plain = jnp.dot(states, q_full, preferred_element_type=jnp.float32)
        mapped = jnp.dot(applied, q_full, preferred_element_type=jnp.float32)
        eigen_values = ritz[window]
        residual = mapped - plain * eigen_values[None, :]
        fixed = (residual / (potential[:, None] + eigen_values[None, :])).astype(jnp.bfloat16)
        partial_value = lax.psum_scatter(
            lax.dot_general(states, fixed, contract, preferred_element_type=jnp.float32).astype(
                jnp.bfloat16
            ),
            "wide",
            scatter_dimension=0,
            tiled=True,
        )
        summed = lax.psum_scatter(partial_value, "narrow", scatter_dimension=1, tiled=True).astype(
            jnp.float32
        )
        rotated_list.append(plain.astype(jnp.bfloat16))
        correction_list.append(fixed)
        margin_list.append(summed * factor)
    return (
        jnp.stack(rotated_list, axis=1),
        jnp.stack(correction_list, axis=1),
        jnp.stack(margin_list, axis=0),
    )


def solution(mesh):
    placed = (
        P(("wide", "narrow"), None),
        P(("wide", "narrow"), None),
        P(None, "wide", "narrow"),
        P(),
        P(("wide", "narrow")),
    )
    return jax.shard_map(
        per_device,
        mesh=mesh,
        in_specs=placed,
        out_specs=(
            P(("wide", "narrow"), None, None),
            P(("wide", "narrow"), None, None),
            P(None, "wide", "narrow"),
        ),
        check_vma=False,
    )
```

profile of v0, /device:TPU:0, one launch (start us, length us, event | category | flops | bytes accessed | tf_op | source)
XLA Modules:
  0.0 160.5 jit_solution(8119105058409660867)
XLA Ops:
  7.2 0.0 copy-start
  7.2 0.0 reduce-scatter.15.cloned.1.call-start
  7.2 0.8 fusion.13
  8.0 0.7 fusion.12
  8.7 10.5 %all-gather.2 = bf16[1,1024,64]{1,2,0:T(8,128)(2,1)S(1)} all-gather(bf16[1,128,64]{1,2,0:T(8,128)(2,1)S(1)} %get-tuple-element.10), channel_id=4, replica_groups=mesh['wide'=8,'narrow'=4] {'wide'}, dimensions={1}, use_global_device_ids=true | all-gather | bytes 147456 | tf_op jit(solution)/shard_map/all_gather | solution.py:18
  19.3 16.3 %all-gather.3 = bf16[1,1024,256]{1,2,0:T(8,128)(2,1)S(1)} all-gather(bf16[1,1024,64]{1,2,0:T(8,128)(2,1)S(1)} %all-gather.2), channel_id=5, replica_groups=mesh['wide'=8,'narrow'=4] {'narrow'}, dimensions={2}, use_global_device_ids=true | all-gather | bytes 655360 | tf_op jit(solution)/shard_map/all_gather | solution.py:19
  35.6 0.0 copy-done
  35.6 0.0 copy-start.1
  35.6 0.5 fusion.7
  36.1 0.0 copy-start.3
  36.1 0.7 copy-done.1
  36.8 0.0 copy-done.3
  36.8 0.5 fusion.4
  37.3 0.5 fusion.3
  37.8 1.0 copy.14
  38.8 0.0 reduce-scatter.15.cloned.1.call-update
  38.8 0.0 reduce-scatter.13.cloned.1.call-start
  38.9 9.0 %all-gather = bf16[1,1024,64]{1,2,0:T(8,128)(2,1)S(1)} all-gather(bf16[1,128,64]{1,2,0:T(8,128)(2,1)S(1)} %get-tuple-element.9), channel_id=2, replica_groups=mesh['wide'=8,'narrow'=4] {'wide'}, dimensions={1}, use_global_device_ids=true | all-gather | bytes 147456 | tf_op jit(solution)/shard_map/all_gather | solution.py:18
  47.9 16.6 %all-gather.1 = bf16[1,1024,256]{1,2,0:T(8,128)(2,1)S(1)} all-gather(bf16[1,1024,64]{1,2,0:T(8,128)(2,1)S(1)} %all-gather), channel_id=3, replica_groups=mesh['wide'=8,'narrow'=4] {'narrow'}, dimensions={2}, use_global_device_ids=true | all-gather | bytes 655360 | tf_op jit(solution)/shard_map/all_gather | solution.py:19
  64.5 0.0 copy-start.2
  64.5 0.5 fusion.10
  65.0 0.7 copy-done.2
  65.7 0.5 fusion.5
  66.2 0.5 fusion.2
  66.6 1.0 copy.12
  67.6 0.0 reduce-scatter.13.cloned.1.call-update
  67.7 0.0 reduce-scatter.11.cloned.1.call-start
  67.8 5.8 %reduce-scatter.15.cloned.1.call-done = bf16[128,256]{1,0:T(8,128)(2,1)} async-done(((bf16[1024,256]{1,0:T(8,128)(2,1)}), bf16[128,256]{1,0:T(8,128)(2,1)}) %reduce-scatter.15.cloned.1.call-update) | async-done | bytes 65552
  73.6 1.6 copy.15
  75.2 0.0 reduce-scatter.11.cloned.1.call-update
  75.2 0.0 reduce-scatter.9.cloned.1.call-start
  75.3 0.1 pad_maximum_fusion
  75.3 1.3 copy.10
  76.7 0.1 pad_maximum_fusion.1
  76.7 1.3 copy.11
  78.0 32.8 %reduce-scatter.13.cloned.1.call-done = bf16[128,256]{1,0:T(8,128)(2,1)} async-done(((bf16[1024,256]{1,0:T(8,128)(2,1)}), bf16[128,256]{1,0:T(8,128)(2,1)}) %reduce-scatter.13.cloned.1.call-update) | async-done | bytes 65552
  110.9 1.6 copy.13
  112.4 0.0 reduce-scatter.9.cloned.1.call-update
  112.5 20.6 %reduce-scatter.11.cloned.1.call-done = bf16[128,64]{0,1:T(8,128)(2,1)} async-done(((bf16[128,256]{0,1:T(8,128)(2,1)}), bf16[128,64]{0,1:T(8,128)(2,1)}) %reduce-scatter.11.cloned.1.call-update) | async-done | bytes 16400 | tf_op jit(solution)/shard_map/reduce_scatter | solution.py:33
  133.0 0.7 multiply_bitcast_fusion
  133.7 18.9 %reduce-scatter.9.cloned.1.call-done = bf16[128,64]{0,1:T(8,128)(2,1)} async-done(((bf16[128,256]{0,1:T(8,128)(2,1)}), bf16[128,64]{0,1:T(8,128)(2,1)}) %reduce-scatter.9.cloned.1.call-update) | async-done | bytes 16400 | tf_op jit(solution)/shard_map/reduce_scatter | solution.py:33
  152.6 0.7 multiply_bitcast_fusion.1
  153.3 0.6 pad_maximum_fusion.2
  (2 shorter events, 0.1 us)
Async XLA Ops:
  7.2 28.4 %copy-start = (bf16[512,1024]{1,0:T(8,128)(2,1)S(1)}, bf16[512,1024]{1,0:T(8,128)(2,1)}, u32[]{:S(2)}) copy-start(bf16[512,1024]{1,0:T(8,128)(2,1)} %param.5) | copy-start | bytes 3145732
  7.2 66.4 %reduce-scatter.15.cloned.1.call-start = ((), (), s32[]{:S(2)}) async-start(), calls=%async_computation.7 | async-start | bytes 589824
  35.6 1.2 copy-start.1
  36.1 0.7 copy-start.3
  38.8 72.1 %reduce-scatter.13.cloned.1.call-start = ((), (), s32[]{:S(2)}) async-start(), calls=%async_computation.6 | async-start | bytes 589824
  64.5 1.2 copy-start.2
  67.7 65.3 %reduce-scatter.11.cloned.1.call-start = ((), (), s32[]{:S(2)}) async-start(), calls=%async_computation.5 | async-start | bytes 81920 | tf_op jit(solution)/shard_map/reduce_scatter | solution.py:33
  75.2 77.4 %reduce-scatter.9.cloned.1.call-start = ((), (), s32[]{:S(2)}) async-start(), calls=%async_computation.4 | async-start | bytes 81920 | tf_op jit(solution)/shard_map/reduce_scatter | solution.py:33
Sparse Core Ops, SparseCore 0:
  38.9 34.6 reduce-scatter.14
  76.7 34.1 reduce-scatter.12
  113.7 19.2 reduce-scatter.10
  135.1 17.4 reduce-scatter.8
where the time goes:
time: 161 us; the launch traced here: 160 us
  waiting for transfers between devices  78.1 us (49%)
  blocking collectives  52.5 us (33%)
  between operations  13.9 us (9%)
  local copies, waits for them, and re-layouts  10.8 us (7%)
  matrix products  2.82 us (2%)
  other arithmetic  2.24 us (1%)
    reduce_scatter x2, waiting for transfers between devices, per_device(): lax.psum_scatter(partial_value, 'narrow', scatter_dimension=1, tiled=True)  39.4 us
    unnamed x6, waiting for transfers between devices  38.7 us
    all_gather x2, blocking collectives, per_device(): q_full = lax.all_gather(q_tall, 'narrow', axis=1, tiled=True)  32.9 us
    all_gather x2, blocking collectives, per_device(): q_tall = lax.all_gather(q_local, 'wide', axis=0, tiled=True)  19.6 us
    unnamed x14, local copies, waits for them, and re-layouts  9.3 us
  transfers between devices with their start and end apart: 4, of which 4 were waited for; matrix products, arithmetic and copies ran while one was open for 6% of the time, Pallas kernels for 0%

commit v1 on v0

--- a/solution.py
+++ b/solution.py
@@ -16,7 +16,15 @@
     for window in range(rotation.shape[0]):
         q_local = rotation[window]
         q_tall = lax.all_gather(q_local, "wide", axis=0, tiled=True)
-        q_full = lax.all_gather(q_tall, "narrow", axis=1, tiled=True)
+        ways, here, step = (lax.axis_size("narrow"), lax.axis_index("narrow"), q_tall.shape[1])
+        line, have = (q_tall, 1)
+        while have < ways:
+            line = jnp.concatenate(
+                [line, lax.ppermute(line, "narrow", [(d, (d - have) % ways) for d in range(ways)])],
+                axis=1,
+            )
+            have = 2 * have
+        q_full = jnp.roll(line, here * step, axis=1)
         plain = jnp.dot(states, q_full, preferred_element_type=jnp.float32)
         mapped = jnp.dot(applied, q_full, preferred_element_type=jnp.float32)
         eigen_values = ritz[window]

time: 161 us -> 185 us (1.15)
  waiting for transfers between devices: 78.1 us -> 129 us
  blocking collectives: 52.5 us -> 19.5 us
  starting transfers between devices: 0.16 us -> 4.36 us
  other arithmetic: 2.24 us -> 4.3 us
    all_gather x2 -> x0, blocking collectives: 32.9 us -> none  [per_device(): q_full = lax.all_gather(q_tall, 'narrow', axis=1, tiled=True)]
    unnamed x6, waiting for transfers between devices: 38.7 us -> 64 us
    ppermute x0 -> x4, waiting for transfers between devices: none -> 25.3 us  [per_device(): lax.ppermute(line, 'narrow', [(d, (d - have) % ways) for d in range(ways)])]
    ppermute x0 -> x4, starting transfers between devices: none -> 4.19 us  [per_device(): lax.ppermute(line, 'narrow', [(d, (d - have) % ways) for d in range(ways)])]
    concatenate x0 -> x3, other arithmetic: none -> 2.05 us  [the longest x1 2.02 us: per_device(): q_full = jnp.roll(line, here * step, axis=1)]
    unnamed x14 -> x20, local copies, waits for them, and re-layouts: 9.3 us -> 10.2 us
  transfers between devices with their start and end apart: 4 -> 8, of which waited for: 4 -> 7; matrix products, arithmetic and copies ran while one was open for 6% -> 5% of each run, Pallas kernels for 0% -> 0%
where the time goes in v1:
time: 185 us
  waiting for transfers between devices  129 us (70%)
  blocking collectives  19.5 us (11%)
  between operations  14 us (8%)
  local copies, waits for them, and re-layouts  11 us (6%)
  starting transfers between devices  4.36 us (2%)
  other arithmetic  4.3 us (2%)
  matrix products  2.8 us (2%)
    unnamed x6, waiting for transfers between devices  64 us
    reduce_scatter x2, waiting for transfers between devices, per_device(): lax.psum_scatter(partial_value, 'narrow', scatter_dimension=1, tiled=True)  39.4 us
    ppermute x4, waiting for transfers between devices, per_device(): lax.ppermute(line, 'narrow', [(d, (d - have) % ways) for d in range(ways)])  25.3 us
    all_gather x2, blocking collectives, per_device(): q_tall = lax.all_gather(q_local, 'wide', axis=0, tiled=True)  19.5 us
    unnamed x20, local copies, waits for them, and re-layouts  10.2 us
    ppermute x4, starting transfers between devices, per_device(): lax.ppermute(line, 'narrow', [(d, (d - have) % ways) for d in range(ways)])  4.19 us
  transfers between devices with their start and end apart: 8, of which 7 were waited for; matrix products, arithmetic and copies ran while one was open for 5% of the time, Pallas kernels for 0%

profile of v1, /device:TPU:0, one launch (start us, length us, event | category | flops | bytes accessed | tf_op | source)
XLA Modules:
  0.0 184.7 jit_solution(4152002219181986047)
XLA Ops:
  7.2 0.0 copy-start
  7.2 0.0 reduce-scatter.13.cloned.1.call-start
  7.2 0.8 fusion.18
  8.0 10.5 %all-gather.1 = bf16[1,1024,64]{1,2,0:T(8,128)(2,1)S(1)} all-gather(bf16[1,128,64]{1,2,0:T(8,128)(2,1)S(1)} %get-tuple-element.11), channel_id=3, replica_groups=mesh['wide'=8,'narrow'=4] {'wide'}, dimensions={1}, use_global_device_ids=true | all-gather | bytes 147456 | tf_op jit(solution)/shard_map/all_gather | solution.py:18
  18.6 3.6 %collective-permute-start.2 = (bf16[1024,64]{0,1:T(8,128)(2,1)S(1)}, bf16[1024,64]{0,1:T(8,128)(2,1)S(1)}, u32[]{:S(2)}, u32[]{:S(2)}) collective-permute-start(bf16[1024,64]{0,1:T(8,128)(2,1)S(1)} %bitcast.48), channel_id=1, source_target_pairs={{0,3},{1,0},{2,1},{3,2},{4,7},{5,4},{6,5},{7,6},{8,11},{9,8},{10,9... | collective-permute-start | bytes 393224 | tf_op jit(solution)/shard_map/ppermute | solution.py:23
  22.2 9.0 %all-gather = bf16[1,1024,64]{1,2,0:T(8,128)(2,1)S(1)} all-gather(bf16[1,128,64]{1,2,0:T(8,128)(2,1)S(1)} %get-tuple-element.10), channel_id=2, replica_groups=mesh['wide'=8,'narrow'=4] {'wide'}, dimensions={1}, use_global_device_ids=true | all-gather | bytes 147456 | tf_op jit(solution)/shard_map/all_gather | solution.py:18
  31.2 0.4 collective-permute-start
  31.7 0.1 collective-permute-start.3
  31.7 6.3 %collective-permute-done = bf16[1024,64]{0,1:T(8,128)(2,1)S(1)} collective-permute-done((bf16[1024,64]{0,1:T(8,128)(2,1)S(1)}, bf16[1024,64]{0,1:T(8,128)(2,1)S(1)}, u32[]{:S(2)}, u32[]{:S(2)}) %collective-permute-start) | collective-permute-done | bytes 131104 | tf_op jit(solution)/shard_map/ppermute | solution.py:23
  38.0 0.1 collective-permute-start.1
  38.1 0.0 copy-start.3
  38.1 0.7 copy-done.3
  38.8 14.3 %collective-permute-done.3 = bf16[1024,128]{0,1:T(8,128)(2,1)S(1)} collective-permute-done((bf16[1024,128]{0,1:T(8,128)(2,1)S(1)}, bf16[1024,128]{0,1:T(8,128)(2,1)S(1)}, u32[]{:S(2)}, u32[]{:S(2)}) %collective-permute-start.3) | collective-permute-done | bytes 262176 | tf_op jit(solution)/shard_map/ppermute | solution.py:23
  53.1 4.7 %collective-permute-done.1 = bf16[1024,128]{0,1:T(8,128)(2,1)S(1)} collective-permute-done((bf16[1024,128]{0,1:T(8,128)(2,1)S(1)}, bf16[1024,128]{0,1:T(8,128)(2,1)S(1)}, u32[]{:S(2)}, u32[]{:S(2)}) %collective-permute-start.1) | collective-permute-done | bytes 262176 | tf_op jit(solution)/shard_map/ppermute | solution.py:23
  57.8 2.0 %fusion.10 = (bf16[1024,256]{0,1:T(8,128)(2,1)S(1)}, bf16[1024,256]{0,1:T(8,128)(2,1)S(1)}) fusion(s32[]{:T(128)S(6)} %select_n.13, bf16[1024,64]{0,1:T(8,128)(2,1)S(1)} %bitcast.50, bf16[1024,64]{0,1:T(8,128)(2,1)S(1)} %collective-permute-done.2, bf16[1024,128]{0,1:T(8,128)(2,1)S(1)} %collective-permute-done.3, ...), kind=kLoop, calls=%fused_computation.26 | loop fusion | flops 6291456 | bytes 2097156 | tf_op jit(solution)/shard_map/jit(_roll_dynamic)/concatenate | solution.py:27
  59.8 0.0 copy-start.4
  59.9 0.5 fusion.20
  60.4 0.7 copy-done.4
  61.1 0.0 copy-done.6
  61.1 0.5 fusion.7
  61.6 0.4 fusion.4
  62.0 1.0 copy.12
  63.0 0.0 reduce-scatter.13.cloned.1.call-update
  63.1 0.0 reduce-scatter.15.cloned.1.call-start
  63.1 0.5 fusion.21
  63.6 0.7 copy-done.5
  64.3 0.5 fusion.6
  64.8 0.7 copy-done.1
  65.5 0.4 fusion.5
  66.0 1.0 copy.14
  67.0 0.0 reduce-scatter.15.cloned.1.call-update
  67.0 0.0 reduce-scatter.9.cloned.1.call-start
  67.1 30.7 %reduce-scatter.13.cloned.1.call-done = bf16[128,256]{1,0:T(8,128)(2,1)} async-done(((bf16[1024,256]{1,0:T(8,128)(2,1)}), bf16[128,256]{1,0:T(8,128)(2,1)}) %reduce-scatter.13.cloned.1.call-update) | async-done | bytes 65552
  97.8 1.6 copy.13
  99.4 0.0 reduce-scatter.9.cloned.1.call-update
  99.4 0.0 reduce-scatter.11.cloned.1.call-start
  99.5 0.1 pad_maximum_fusion
  99.6 1.1 copy.10
  100.7 0.1 pad_maximum_fusion.1
  100.7 1.1 copy.11
  101.8 33.3 %reduce-scatter.15.cloned.1.call-done = bf16[128,256]{1,0:T(8,128)(2,1)} async-done(((bf16[1024,256]{1,0:T(8,128)(2,1)}), bf16[128,256]{1,0:T(8,128)(2,1)}) %reduce-scatter.15.cloned.1.call-update) | async-done | bytes 65552
  135.1 1.6 copy.15
  136.7 0.0 reduce-scatter.11.cloned.1.call-update
  136.7 20.0 %reduce-scatter.9.cloned.1.call-done = bf16[128,64]{0,1:T(8,128)(2,1)} async-done(((bf16[128,256]{0,1:T(8,128)(2,1)}), bf16[128,64]{0,1:T(8,128)(2,1)}) %reduce-scatter.9.cloned.1.call-update) | async-done | bytes 16400 | tf_op jit(solution)/shard_map/reduce_scatter | solution.py:41
  156.7 0.7 multiply_bitcast_fusion.1
  157.4 19.5 %reduce-scatter.11.cloned.1.call-done = bf16[128,64]{0,1:T(8,128)(2,1)} async-done(((bf16[128,256]{0,1:T(8,128)(2,1)}), bf16[128,64]{0,1:T(8,128)(2,1)}) %reduce-scatter.11.cloned.1.call-update) | async-done | bytes 16400 | tf_op jit(solution)/shard_map/reduce_scatter | solution.py:41
  176.8 0.7 multiply_bitcast_fusion
  177.6 0.6 pad_maximum_fusion.4
  (12 shorter events, 0.1 us)
Async XLA Ops:
  7.2 52.7 %copy-start = (bf16[512,1024]{1,0:T(8,128)(2,1)S(1)}, bf16[512,1024]{1,0:T(8,128)(2,1)}, u32[]{:S(2)}) copy-start(bf16[512,1024]{1,0:T(8,128)(2,1)} %param.7) | copy-start | bytes 3145732
  7.2 90.7 %reduce-scatter.13.cloned.1.call-start = ((), (), s32[]{:S(2)}) async-start(), calls=%async_computation.6 | async-start | bytes 589824
  18.6 13.1 %collective-permute-start.2 = (bf16[1024,64]{0,1:T(8,128)(2,1)S(1)}, bf16[1024,64]{0,1:T(8,128)(2,1)S(1)}, u32[]{:S(2)}, u32[]{:S(2)}) collective-permute-start(bf16[1024,64]{0,1:T(8,128)(2,1)S(1)} %bitcast.48), channel_id=1, source_target_pairs={{0,3},{1,0},{2,1},{3,2},{4,7},{5,4},{6,5},{7,6},{8,11},{9,8},{10,9... | collective-permute-start | bytes 393224 | tf_op jit(solution)/shard_map/ppermute | solution.py:23
  31.2 6.8 %collective-permute-start = (bf16[1024,64]{0,1:T(8,128)(2,1)S(1)}, bf16[1024,64]{0,1:T(8,128)(2,1)S(1)}, u32[]{:S(2)}, u32[]{:S(2)}) collective-permute-start(bf16[1024,64]{0,1:T(8,128)(2,1)S(1)} %bitcast.51), channel_id=1, source_target_pairs={{0,3},{1,0},{2,1},{3,2},{4,7},{5,4},{6,5},{7,6},{8,11},{9,8},{10,9... | collective-permute-start | bytes 393224 | tf_op jit(solution)/shard_map/ppermute | solution.py:23
  31.7 21.4 %collective-permute-start.3 = (bf16[1024,128]{0,1:T(8,128)(2,1)S(1)}, bf16[1024,128]{0,1:T(8,128)(2,1)S(1)}, u32[]{:S(2)}, u32[]{:S(2)}) collective-permute-start(bf16[1024,128]{0,1:T(8,128)(2,1)S(1)} %pad_maximum_fusion.3), channel_id=1, source_target_pairs={{0,2},{1,3},{2,0},{3,1},{4,6},{5,7},{6,4},{7,5},{8,10},{9,11},{10,... | collective-permute-start | bytes 786440 | tf_op jit(solution)/shard_map/ppermute | solution.py:23
  38.0 19.8 %collective-permute-start.1 = (bf16[1024,128]{0,1:T(8,128)(2,1)S(1)}, bf16[1024,128]{0,1:T(8,128)(2,1)S(1)}, u32[]{:S(2)}, u32[]{:S(2)}) collective-permute-start(bf16[1024,128]{0,1:T(8,128)(2,1)S(1)} %pad_maximum_fusion.2), channel_id=1, source_target_pairs={{0,2},{1,3},{2,0},{3,1},{4,6},{5,7},{6,4},{7,5},{8,10},{9,11},{10,... | collective-permute-start | bytes 786440 | tf_op jit(solution)/shard_map/ppermute | solution.py:23
  38.1 0.7 copy-start.3
  59.8 1.2 copy-start.4
  60.3 0.7 copy-start.6
  63.1 72.0 %reduce-scatter.15.cloned.1.call-start = ((), (), s32[]{:S(2)}) async-start(), calls=%async_computation.7 | async-start | bytes 589824
  63.1 1.2 copy-start.5
  64.8 0.7 copy-start.1
  67.0 89.7 %reduce-scatter.9.cloned.1.call-start = ((), (), s32[]{:S(2)}) async-start(), calls=%async_computation.4 | async-start | bytes 81920 | tf_op jit(solution)/shard_map/reduce_scatter | solution.py:41
  99.4 77.4 %reduce-scatter.11.cloned.1.call-start = ((), (), s32[]{:S(2)}) async-start(), calls=%async_computation.5 | async-start | bytes 81920 | tf_op jit(solution)/shard_map/reduce_scatter | solution.py:41
  99.5 1.1 copy-start.2
Sparse Core Ops, SparseCore 0:
  63.2 34.6 reduce-scatter.12
  100.9 34.1 reduce-scatter.14
  137.3 19.2 reduce-scatter.8
  159.3 17.4 reduce-scatter.10
